TPU v7x, 32 devices: a whole 2x2x4 slice. The times are simulated.
32 devices in a mesh: pages: 2 (over y), tile: 4 (over z), mp: 2 (over x), batch: 2 (over core).
Axes of the slice: x: 2, y: 2, z: 4, core: 2. Of those that a mesh axis runs over, the one named last changes fastest.
Arguments:
- page_cells: bfloat16 [4, 48, 24, 1024], P(('pages', 'batch'), 'tile'), parts along dimension 0, may hold values from -40 to 40
- text_states: bfloat16 [4, 1024, 1024], P(('pages', 'batch'), 'tile'), parts along dimension 0, may hold values from -40 to 40
- enc_query: bfloat16 [1024, 1024], P('batch', 'mp'), may hold values from -2.5 to 2.5
- enc_keyval: bfloat16 [1024, 2, 1024], P('batch', None, 'mp'), may hold values from -0.1875 to 0.1875
- enc_proj: bfloat16 [1024, 1024], P('mp', 'batch'), may hold values from -0.1875 to 0.1875
- dec_query: bfloat16 [1024, 1024], P('batch', 'mp'), may hold values from -2.5 to 2.5
- dec_keyval: bfloat16 [1024, 2, 1024], P('batch', None, 'mp'), may hold values from -0.1875 to 0.1875
- dec_out: bfloat16 [1024, 1024], P('mp', 'batch'), may hold values from -0.1875 to 0.1875
Outputs:
- encoded: bfloat16 [4, 48, 24, 1024], P(('pages', 'batch'), 'tile'), parts along dimension 0
- decoded: bfloat16 [4, 1024, 1024], P(('pages', 'batch'), ('tile', 'mp')), parts along dimension 0
There are 2 independent parts, one for each index of `pages`. A program takes and returns all parts, laid end to end along the dimension named above; an argument that names none is the same for every part. Nothing has to cross between parts.
All inputs are finite; a program needn't handle non-finite values.
Results may differ from a plain program's by a relative error of at most 0.012.
Values may be sent and summed in bfloat16 or wider, within the bound.
No kernel may reach another device: no remote copies, remote signals or barrier semaphores. Data moves between devices by JAX's collectives and lax.ppermute only.
A program may use at most 64 MiB of HBM per device.

v0:
```python
import math
import jax
import jax.numpy as jnp
from jax import lax
from jax.sharding import PartitionSpec as P

HEAD_ENC = 32
HEAD_DEC = 64


def from_behind(value, axis, by):
    devices = lax.axis_size(axis)
    return lax.ppermute(value, axis, [(i, (i + by) % devices) for i in range(devices)])


def layer_norm(values):
    center = values - jnp.mean(values, axis=-1, keepdims=True)
    variance = jnp.mean(center * center, axis=-1, keepdims=True)
    return center / jnp.sqrt(variance + 1e-05)


def regions(length, window, offset):
    index_row = jnp.arange(length, dtype=jnp.int32)
    return jnp.where(
        index_row < length - window, 0, jnp.where(index_row < length - offset, 1, 2)
    ).astype(jnp.int32)


def body(page_cells, text_states, enc_query, enc_keyval, enc_proj, dec_query, dec_keyval, dec_out):
    wq_enc, wkv_enc, wproj_enc, wq_dec, wkv_dec, wout_dec = (
        lax.all_gather(enc_query, "batch", axis=0, tiled=True),
        lax.all_gather(enc_keyval, "batch", axis=0, tiled=True),
        lax.all_gather(enc_proj, "batch", axis=1, tiled=True),
        lax.all_gather(dec_query, "batch", axis=0, tiled=True),
        lax.all_gather(dec_keyval, "batch", axis=0, tiled=True),
        lax.all_gather(dec_out, "batch", axis=1, tiled=True),
    )
    pages_here, window, columns, width = page_cells.shape
    offset = window // 2
    own_rows = window * columns
    hq_enc = wq_enc.shape[1]
    heads_enc = hq_enc // HEAD_ENC
    joined = jnp.concatenate([wq_enc, wkv_enc.reshape(width, 2 * hq_enc)], axis=1)
    rows_below = from_behind(page_cells[:, :offset], "tile", -1)
    normed = layer_norm(
        jnp.concatenate([page_cells[:, offset:], rows_below], axis=1).astype(jnp.float32)
    ).astype(jnp.bfloat16)
    projected = jnp.einsum(
        "prcd,de->prce", normed, joined, preferred_element_type=jnp.float32
    ).astype(jnp.bfloat16)
    projected = jnp.roll(projected, -offset, axis=2)
    per_row = columns // window
    shaped = projected.reshape(pages_here, window, per_row, window, 3, heads_enc, HEAD_ENC)
    shaped = jnp.swapaxes(shaped, 1, 2).reshape(
        pages_here, per_row, window * window, 3, heads_enc, HEAD_ENC
    )
    win_q = shaped[:, :, :, 0]
    win_k = shaped[:, :, :, 1]
    win_v = shaped[:, :, :, 2]
    is_last = lax.axis_index("tile") == lax.axis_size("tile") - 1
    local_rows = jnp.arange(window, dtype=jnp.int32)
    row_region = jnp.where(is_last, jnp.where(local_rows < window - offset, 1, 2), 0).astype(
        jnp.int32
    )
    labels = row_region[:, None] * 3 + regions(columns, window, offset)[None, :]
    labels = jnp.swapaxes(labels.reshape(window, per_row, window), 0, 1).reshape(
        per_row, window * window
    )
    allowed = labels[:, :, None] == labels[:, None, :]
    win_scores = jnp.einsum(
        "pnqhd,pnkhd->pnhqk", win_q, win_k, preferred_element_type=jnp.float32
    ) / math.sqrt(HEAD_ENC)
    win_scores = jnp.where(allowed[None, :, None], win_scores, -jnp.inf)
    top = jnp.max(win_scores, axis=-1, keepdims=True)
    expd = jnp.exp(win_scores - top)
    win_weights = (expd / jnp.sum(expd, axis=-1, keepdims=True)).astype(jnp.bfloat16)
    win_out = jnp.einsum(
        "pnhqk,pnkhd->pnqhd", win_weights, win_v, preferred_element_type=jnp.float32
    ).astype(jnp.bfloat16)
    win_out = win_out.reshape(pages_here, per_row, window, window, hq_enc)
    win_out = jnp.swapaxes(win_out, 1, 2).reshape(pages_here, window, columns, hq_enc)
    win_out = jnp.roll(win_out, offset, axis=2)
    rows_above = from_behind(win_out[:, window - offset :], "tile", 1)
    unrolled = jnp.concatenate([rows_above, win_out[:, : window - offset]], axis=1)
    partial_proj = jnp.einsum(
        "prce,ed->prcd", unrolled, wproj_enc, preferred_element_type=jnp.float32
    )
    summed = lax.psum(partial_proj.astype(jnp.bfloat16), "mp").astype(jnp.float32)
    encoded = (page_cells.astype(jnp.float32) + summed).astype(jnp.bfloat16)
    hq_dec = wq_dec.shape[1]
    heads_dec = hq_dec // HEAD_DEC
    page_normed = (
        layer_norm(encoded.astype(jnp.float32))
        .astype(jnp.bfloat16)
        .reshape(pages_here, own_rows, width)
    )
    page_kv = jnp.einsum(
        "pnd,de->pne",
        page_normed,
        wkv_dec.reshape(width, 2 * hq_dec),
        preferred_element_type=jnp.float32,
    ).astype(jnp.bfloat16)
    text_normed = layer_norm(text_states.astype(jnp.float32)).astype(jnp.bfloat16)
    queries = jnp.einsum(
        "ptd,de->pte", text_normed, wq_dec, preferred_element_type=jnp.float32
    ).astype(jnp.bfloat16)
    text_len = text_states.shape[1]
    query_heads = queries.reshape(pages_here, text_len, heads_dec, HEAD_DEC)
    start_state = (
        jnp.full((pages_here, heads_dec, text_len), -jnp.inf, jnp.float32),
        jnp.zeros((pages_here, heads_dec, text_len), jnp.float32),
        jnp.zeros((pages_here, heads_dec, text_len, HEAD_DEC), jnp.float32),
    )
    carried = start_state
    shard_rows = lax.all_gather(page_kv, "tile", axis=1, tiled=True)
    count = shard_rows.shape[1] // own_rows
    grouped = max(
        (
            factor
            for factor in range(1, count + 1)
            if count % factor == 0 and factor * own_rows <= 2048
        )
    )
    blocks = jnp.moveaxis(
        shard_rows.reshape(pages_here, count // grouped, grouped * own_rows, 2 * hq_dec), 1, 0
    )

    def advance(running, block_kv):
        maxima, totals, accum = running
        span = block_kv.shape[1]
        block_keys = block_kv[..., :hq_dec].reshape(pages_here, span, heads_dec, HEAD_DEC)
        block_vals = block_kv[..., hq_dec:].reshape(pages_here, span, heads_dec, HEAD_DEC)
        cross_scores = jnp.einsum(
            "pqhd,pkhd->phqk", query_heads, block_keys, preferred_element_type=jnp.float32
        ) / math.sqrt(HEAD_DEC)
        newest = jnp.maximum(maxima, jnp.max(cross_scores, axis=-1))
        rescale = jnp.exp(maxima - newest)
        expo = jnp.exp(cross_scores - newest[..., None])
        totals = totals * rescale + jnp.sum(expo, axis=-1)
        accum = accum * rescale[..., None] + jnp.einsum(
            "phqk,pkhd->phqd",
            expo.astype(jnp.bfloat16),
            block_vals,
            preferred_element_type=jnp.float32,
        )
        return ((newest, totals, accum), None)

    carried, unused = lax.scan(advance, carried, blocks)
    maxima, totals, accum = carried
    context = (
        jnp.transpose(accum / totals[..., None], (0, 2, 1, 3))
        .reshape(pages_here, text_len, hq_dec)
        .astype(jnp.bfloat16)
    )
    share = text_len // lax.axis_size("mp")
    mixed = lax.psum_scatter(
        jnp.einsum("pte,ed->tpd", context, wout_dec, preferred_element_type=jnp.float32).astype(
            jnp.bfloat16
        ),
        "mp",
        scatter_dimension=0,
        tiled=True,
    ).astype(jnp.float32)
    own_text = lax.dynamic_slice_in_dim(text_states, lax.axis_index("mp") * share, share, 1)
    decoded = (own_text.astype(jnp.float32) + jnp.moveaxis(mixed, 0, 1)).astype(jnp.bfloat16)
    return (encoded, decoded)


def solution(mesh):
    placed = (
        P(("pages", "batch"), "tile", None, None),
        P(("pages", "batch"), "tile", None),
        P("batch", "mp"),
        P("batch", None, "mp"),
        P("mp", "batch"),
        P("batch", "mp"),
        P("batch", None, "mp"),
        P("mp", "batch"),
    )
    return jax.shard_map(
        body,
        mesh=mesh,
        in_specs=placed,
        out_specs=(
            P(("pages", "batch"), "tile", None, None),
            P(("pages", "batch"), ("tile", "mp"), None),
        ),
        check_vma=False,
    )
```

profile of v0, /device:TPU:0, one launch (start us, length us, event | category | flops | bytes accessed | tf_op | source)
XLA Modules:
  0.0 199.5 jit_solution(16749749369688853707)
XLA Ops:
  7.2 0.7 all-gather.11.cloned.1.call-update
  8.0 0.7 all-gather.9.cloned.1.call-update
  8.7 0.7 all-gather.13.cloned.1.call-update
  9.6 5.1 %collective-permute-start = (bf16[1,6,24,1024]{3,2,1,0:T(8,128)(2,1)S(1)}, bf16[1,6,24,1024]{3,2,1,0:T(8,128)(2,1)S(1)}, u32[]{:S(2)}, u32[]{:S(2)}) collective-permute-start(bf16[1,6,24,1024]{3,2,1,0:T(8,128)(2,1)S(1)} %get-tuple-element.29), channel_id=1, source_target_pairs={{0,12},{4,0},{8,4},{12,8},{1,13},{5,1},{9,5},{13,9},{2,14},{6,2},{... | collective-permute-start | bytes 884744 | tf_op jit(solution)/shard_map/ppermute | solution.py:13
  15.0 0.7 broadcast_compare_fusion
  15.8 5.1 %collective-permute-done = bf16[1,6,24,1024]{3,2,1,0:T(8,128)(2,1)S(1)} collective-permute-done((bf16[1,6,24,1024]{3,2,1,0:T(8,128)(2,1)S(1)}, bf16[1,6,24,1024]{3,2,1,0:T(8,128)(2,1)S(1)}, u32[]{:S(2)}, u32[]{:S(2)}) %collective-permute-start) | collective-permute-done | bytes 294944 | tf_op jit(solution)/shard_map/ppermute | solution.py:13
  21.1 0.3 fusion.31
  21.4 1.5 all-gather.11.cloned.1.call-done
  22.9 2.1 %copy.40 = bf16[128,8,2,512]{3,1,2,0:T(8,128)(2,1)S(1)} copy(bf16[128,8,2,512]{3,2,1,0:T(2,128)(2,1)} %bitcast.102) | data formatting | bytes 4194304
  25.1 9.6 %all-gather.9.cloned.1.call-done = bf16[1024,512]{1,0:T(8,128)(2,1)} async-done(((bf16[512,512]{1,0:T(8,128)(2,1)}), bf16[1024,512]{1,0:T(8,128)(2,1)}) %all-gather.9.cloned.1.call-update) | async-done | bytes 1048592 | tf_op jit(solution)/shard_map/all_gather | solution.py:31
  34.7 2.4 %fusion.12 = bf16[1,12,24,1536]{3,2,1,0:T(8,128)(2,1)S(1)} fusion(bf16[1024,1024]{1,0:T(8,128)(2,1)S(1)} %bitcast.104, bf16[1024,512]{1,0:T(8,128)(2,1)} %all-gather.9.cloned.1.call-done, bf16[6,24,1024]{2,1,0:T(8,128)(2,1)S(1)} %bitcast.106, bf16[6,24,1024]{2,1,0:T(8,128)(2,1)S(1)} %get-tuple-element.28, f32[12,24]{1,0:T(8,128)S(1)} %add_sqrt_fusion.1, ...), kind=kOutput, calls=%fused_computation.17 | convolution fusion | flops 914178048 | bytes 4622592 | tf_op jit(solution)/shard_map/prcd,de->prce/dot_general | solution.py:48
  37.4 1.1 pad_maximum_fusion
  38.5 3.7 %reshape.311 = bf16[1,12,2,12,3,16,32]{6,5,4,3,2,1,0:T(8,128)(2,1)S(1)} reshape(bf16[1,12,24,1536]{3,2,1,0:T(8,128)(2,1)} %pad_maximum_fusion) | data formatting | bytes 1769472 | tf_op jit(solution)/shard_map/reshape | solution.py:53
  42.1 0.6 copy.26
  42.8 0.6 fusion.78
  43.4 1.7 copy.39
  45.1 1.0 copy.38
  46.2 1.0 copy.37
  47.2 4.0 %fusion.81 = (f32[2,16,144]{2,1,0:T(8,128)S(1)}, f32[2,16,144,144]{2,3,1,0:T(8,128)}) fusion(pred[2,144,144]{1,2,0:T(8,128)(4,1)S(1)} %copy-done.8, bf16[1,2,144,1,16,32]{2,5,4,1,3,0:T(8,128)(2,1)S(1)} %copy-done.7, bf16[1,2,144,1,16,32]{2,5,4,1,3,0:T(8,128)(2,1)S(1)} %copy.38), kind=kOutput, calls=%fused_computation.103 | convolution fusion | flops 45121680 | bytes 3303936 | tf_op jit(solution)/shard_map/sub | solution.py:75
  51.2 2.8 %fusion.23 = bf16[1,2,144,16,32]{2,4,3,1,0:T(8,128)(2,1)S(1)} fusion(f32[2,16,144,144]{2,3,1,0:T(8,128)} %get-tuple-element.33, f32[2,16,144]{2,1,0:T(8,128)S(1)} %get-tuple-element.32, bf16[1,2,144,1,16,32]{2,5,4,1,3,0:T(8,128)(2,1)S(1)} %copy.37), kind=kOutput, calls=%fused_computation.37 | convolution fusion | flops 43941888 | bytes 3262464 | tf_op jit(solution)/shard_map/pnhqk,pnkhd->pnqhd/dot_general | solution.py:77
  54.0 1.1 copy.31
  55.1 0.9 reshape.316
  56.2 1.8 collective-permute-start.1
  58.0 6.2 %collective-permute-done.1 = bf16[1,6,24,512]{3,2,1,0:T(8,128)(2,1)S(1)} collective-permute-done((bf16[1,6,24,512]{3,2,1,0:T(8,128)(2,1)S(1)}, bf16[1,6,24,512]{3,2,1,0:T(8,128)(2,1)S(1)}, u32[]{:S(2)}, u32[]{:S(2)}) %collective-permute-start.1) | collective-permute-done | bytes 147488 | tf_op jit(solution)/shard_map/ppermute | solution.py:13
  64.1 2.5 %fusion.20 = bf16[1,12,24,1024]{3,2,1,0:T(8,128)(2,1)} fusion(bf16[512,1024]{1,0:T(8,128)(2,1)} %all-gather.13.cloned.1.call-done, bf16[1,12,18,512]{3,2,1,0:T(8,128)(2,1)S(1)} %bitcast.99, bf16[1,12,6,512]{3,2,1,0:T(8,128)(2,1)S(1)} %slice.63, bf16[1,6,24,512]{3,2,1,0:T(8,128)(2,1)S(1)} %collective-permute-done.1), kind=kOutput, calls=%fused_computation.34 | convolution fusion | flops 303169536 | bytes 2080768 | tf_op jit(solution)/shard_map/prce,ed->prcd/dot_general | solution.py:85
  66.7 0.5 all-gather.15.cloned.1.call-update
  67.5 3.6 %copy.41 = bf16[128,8,2,512]{3,1,2,0:T(8,128)(2,1)} copy(bf16[128,8,2,512]{3,2,1,0:T(2,128)(2,1)} %bitcast.101) | data formatting | bytes 4194304
  71.1 25.1 %all-reduce.2.cloned.1.call-done = bf16[1,12,24,1024]{3,2,1,0:T(8,128)(2,1)} async-done(((bf16[1,12,24,1024]{3,2,1,0:T(8,128)(2,1)}), bf16[1,12,24,1024]{3,2,1,0:T(8,128)(2,1)}) %all-reduce.2.cloned.1.call-update) | async-done | bytes 589840 | tf_op jit(solution)/shard_map/psum | solution.py:88
  96.2 1.5 convert_reduce_fusion
  97.7 0.3 fusion.28
  98.0 0.2 fusion.29
  98.3 1.6 convolution_convert_fusion
  99.9 0.7 all-gather.19.cloned.1.call-update
  100.8 0.3 fusion.34
  101.1 5.6 %all-gather.15.cloned.1.call-done = bf16[1024,512]{1,0:T(8,128)(2,1)} async-done(((bf16[512,512]{1,0:T(8,128)(2,1)}), bf16[1024,512]{1,0:T(8,128)(2,1)}) %all-gather.15.cloned.1.call-update) | async-done | bytes 1048592 | tf_op jit(solution)/shard_map/all_gather | solution.py:34
  106.8 1.7 convolution_convert_fusion.3
  108.5 0.8 copy.33
  109.3 50.8 %all-gather.21.cloned.1.call-done = bf16[1152,1024]{1,0:T(8,128)(2,1)} async-done(((bf16[288,1024]{1,0:T(8,128)(2,1)}), bf16[1152,1024]{1,0:T(8,128)(2,1)}) %all-gather.21.cloned.1.call-update) | async-done | bytes 2359312 | tf_op jit(solution)/shard_map/all_gather | solution.py:115
  160.1 1.8 fusion.79
  161.9 0.7 copy.34
  162.6 2.5 %multiply_reduce_fusion = (f32[8,256]{1,0:T(8,128)S(1)}, f32[8,256,1152]{2,1,0:T(8,128)S(1)}) fusion(bf16[256,8,64]{0,2,1:T(8,128)(2,1)} %bitcast.108, bf16[1152,8,64]{0,2,1:T(8,128)(2,1)S(1)} %bitcast.97), kind=kOutput, calls=%fused_computation.2 | convolution fusion | flops 306706432 | bytes 10887168 | tf_op jit(solution)/shard_map/while/body/eval_jaxpr/pqhd,pkhd->phqk/dot_general | solution.py:133
  165.1 1.9 fusion.1
  167.0 1.7 copy-done
  168.7 0.7 copy.35
  169.4 5.5 %fusion.40 = bf16[8,256,64]{1,2,0:T(8,128)(2,1)S(1)} fusion(bf16[1152,8,64]{0,2,1:T(8,128)(2,1)S(1)} %bitcast.105, f32[8,256,1152]{2,1,0:T(8,128)} %copy-done, f32[8,256]{1,0:T(8,128)S(1)} %get-tuple-element.34, f32[8,256]{1,0:T(8,128)S(1)} %get-tuple-element.31, f32[8,256]{1,0:T(8,128)S(1)} %get-tuple-element.30), kind=kOutput, calls=%fused_computation.52 | convolution fusion | flops 309460992 | bytes 10903552 | tf_op jit(solution)/shard_map/while/body/eval_jaxpr/phqk,pkhd->phqd/dot_general | solution.py:140
  175.0 2.5 %fusion.24 = bf16[256,1,1024]{2,0,1:T(8,128)(2,1)} fusion(bf16[256,512]{0,1:T(8,128)(2,1)S(1)} %bitcast.110, bf16[512,1024]{1,0:T(8,128)(2,1)} %all-gather.19.cloned.1.call-done), kind=kOutput, calls=%fused_computation.38 | convolution fusion | flops 268697600 | bytes 1835008 | tf_op jit(solution)/shard_map/pte,ed->tpd/dot_general | solution.py:157
  177.6 13.6 %reduce-scatter.2.cloned.1.call-done = bf16[128,1,1024]{2,0,1:T(8,128)(2,1)} async-done(((bf16[256,1,1024]{2,0,1:T(8,128)(2,1)}), bf16[128,1,1024]{2,0,1:T(8,128)(2,1)}) %reduce-scatter.2.cloned.1.call-update) | async-done | bytes 262160 | tf_op jit(solution)/shard_map/reduce_scatter | solution.py:156
  191.2 1.7 fusion.50
  (56 shorter events, 1.8 us)
Async XLA Ops:
  7.2 2.3 %copy-start.4 = (bf16[1,12,24,1024]{3,2,1,0:T(8,128)(2,1)S(1)}, bf16[1,12,24,1024]{3,2,1,0:T(8,128)(2,1)}, u32[]{:S(2)}) copy-start(bf16[1,12,24,1024]{3,2,1,0:T(8,128)(2,1)} %param.8) | copy-start | bytes 1769476
  7.2 15.8 %all-gather.11.cloned.1.call-start = ((), (), s32[]{:S(2)}) async-start(), calls=%async_computation.2 | async-start | bytes 3145728 | tf_op jit(solution)/shard_map/all_gather | solution.py:32
  7.9 26.8 %all-gather.9.cloned.1.call-start = ((), (), s32[]{:S(2)}) async-start(), calls=%async_computation.1 | async-start | bytes 1572864 | tf_op jit(solution)/shard_map/all_gather | solution.py:31
  8.7 49.3 %all-gather.13.cloned.1.call-start = ((), (), s32[]{:S(2)}) async-start(), calls=%async_computation.3 | async-start | bytes 1572864 | tf_op jit(solution)/shard_map/all_gather | solution.py:33
  9.4 58.1 %all-gather.17.cloned.1.call-start = ((), (), s32[]{:S(2)}) async-start(), calls=%async_computation.6 | async-start | bytes 3145728 | tf_op jit(solution)/shard_map/all_gather | solution.py:35
  9.6 11.4 %collective-permute-start = (bf16[1,6,24,1024]{3,2,1,0:T(8,128)(2,1)S(1)}, bf16[1,6,24,1024]{3,2,1,0:T(8,128)(2,1)S(1)}, u32[]{:S(2)}, u32[]{:S(2)}) collective-permute-start(bf16[1,6,24,1024]{3,2,1,0:T(8,128)(2,1)S(1)} %get-tuple-element.29), channel_id=1, source_target_pairs={{0,12},{4,0},{8,4},{12,8},{1,13},{5,1},{9,5},{13,9},{2,14},{6,2},{... | collective-permute-start | bytes 884744 | tf_op jit(solution)/shard_map/ppermute | solution.py:13
  14.7 81.5 %all-reduce.2.cloned.1.call-start = ((), (), s32[]{:S(2)}) async-start(), calls=%async_computation.4 | async-start | bytes 1179648 | tf_op jit(solution)/shard_map/psum | solution.py:88
  45.1 2.1 %copy-start.7 = (bf16[1,2,144,1,16,32]{2,5,4,1,3,0:T(8,128)(2,1)S(1)}, bf16[1,2,144,1,16,32]{2,5,4,1,3,0:T(8,128)(2,1)}, u32[]{:S(2)}) copy-start(bf16[1,2,144,1,16,32]{2,5,4,1,3,0:T(8,128)(2,1)} %copy.39) | copy-start | bytes 884740
  45.1 2.1 %copy-start.8 = (pred[2,144,144]{1,2,0:T(8,128)(4,1)S(1)}, pred[2,144,144]{1,2,0:T(8,128)(4,1)}, u32[]{:S(2)}) copy-start(pred[2,144,144]{1,2,0:T(8,128)(4,1)} %broadcast_compare_fusion) | copy-start | bytes 124420
  56.2 8.0 %collective-permute-start.1 = (bf16[1,6,24,512]{3,2,1,0:T(8,128)(2,1)S(1)}, bf16[1,6,24,512]{3,2,1,0:T(8,128)(2,1)S(1)}, u32[]{:S(2)}, u32[]{:S(2)}) collective-permute-start(bf16[1,6,24,512]{3,2,1,0:T(8,128)(2,1)S(1)} %fusion.70), channel_id=1, source_target_pairs={{0,4},{4,8},{8,12},{12,0},{1,5},{5,9},{9,13},{13,1},{2,6},{6,10},{... | collective-permute-start | bytes 442376 | tf_op jit(solution)/shard_map/ppermute | solution.py:13
  66.7 40.1 %all-gather.15.cloned.1.call-start = ((), (), s32[]{:S(2)}) async-start(), calls=%async_computation.5 | async-start | bytes 1572864 | tf_op jit(solution)/shard_map/all_gather | solution.py:34
  67.3 92.8 %all-gather.21.cloned.1.call-start = ((), (), s32[]{:S(2)}) async-start(), calls=%async_computation.9 | async-start | bytes 2949120 | tf_op jit(solution)/shard_map/all_gather | solution.py:115
  67.5 28.7 %copy-start.5 = (bf16[1,12,24,1024]{3,2,1,0:T(8,128)(2,1)S(1)}, bf16[1,12,24,1024]{3,2,1,0:T(8,128)(2,1)}, u32[]{:S(2)}) copy-start(bf16[1,12,24,1024]{3,2,1,0:T(8,128)(2,1)} %param.8) | copy-start | bytes 1769476
  96.2 2.0 %copy-start.6 = (bf16[128,8,2,512]{3,1,2,0:T(8,128)(2,1)S(1)}, bf16[128,8,2,512]{3,1,2,0:T(8,128)(2,1)}, u32[]{:S(2)}) copy-start(bf16[128,8,2,512]{3,1,2,0:T(8,128)(2,1)} %copy.41) | copy-start | bytes 6291460
  97.7 2.2 %copy-start.1 = (bf16[1,12,24,1024]{3,2,1,0:T(8,128)(2,1)}, bf16[1,12,24,1024]{3,2,1,0:T(8,128)(2,1)S(1)}, u32[]{:S(2)}) copy-start(bf16[1,12,24,1024]{3,2,1,0:T(8,128)(2,1)S(1)} %get-tuple-element.15) | copy-start | bytes 1769476
  98.2 2.4 %copy-start.2 = (bf16[1,256,1024]{2,1,0:T(8,128)(2,1)S(1)}, bf16[1,256,1024]{2,1,0:T(8,128)(2,1)}, u32[]{:S(2)}) copy-start(bf16[1,256,1024]{2,1,0:T(8,128)(2,1)} %param.9) | copy-start | bytes 1572868
  99.9 75.1 %all-gather.19.cloned.1.call-start = ((), (), s32[]{:S(2)}) async-start(), calls=%async_computation.7 | async-start | bytes 1572864 | tf_op jit(solution)/shard_map/all_gather | solution.py:36
  100.6 90.6 %reduce-scatter.2.cloned.1.call-start = ((), (), s32[]{:S(2)}) async-start(), calls=%async_computation.8 | async-start | bytes 786432 | tf_op jit(solution)/shard_map/reduce_scatter | solution.py:156
  165.1 3.7 %copy-start = (f32[8,256,1152]{2,1,0:T(8,128)}, f32[8,256,1152]{2,1,0:T(8,128)S(1)}, u32[]{:S(2)}) copy-start(f32[8,256,1152]{2,1,0:T(8,128)S(1)} %get-tuple-element.35) | copy-start | bytes 28311556
  175.0 16.3 %copy-start.3 = (bf16[1,256,1024]{2,1,0:T(8,128)(2,1)S(1)}, bf16[1,256,1024]{2,1,0:T(8,128)(2,1)}, u32[]{:S(2)}) copy-start(bf16[1,256,1024]{2,1,0:T(8,128)(2,1)} %param.9) | copy-start | bytes 1572868
Sparse Core Ops, SparseCore 0:
  9.6 13.3 all-gather.10
  24.5 10.1 all-gather.8
  36.3 10.1 all-gather.12
  47.9 11.7 all-gather.16
  66.8 29.3 all-reduce.1
  97.7 9.0 all-gather.14
  108.4 51.6 all-gather.20
  161.7 7.8 all-gather.18
  177.7 13.4 reduce-scatter.1
where the time goes:
time: 200 us; the launch traced here: 199 us
  waiting for transfers between devices  121 us (60%)
  matrix products  25.6 us (13%)
  local copies, waits for them, and re-layouts  22.9 us (11%)
  between operations  14.2 us (7%)
  other arithmetic  8.42 us (4%)
  starting transfers between devices  7.43 us (4%)
    all_gather x1, waiting for transfers between devices, body(): shard_rows = lax.all_gather(page_kv, 'tile', axis=1, tiled=True)  50.8 us
    psum x1, waiting for transfers between devices, body(): lax.psum(partial_proj.astype(jnp.bfloat16), 'mp').astype(jnp.float32)  25.1 us
    reduce_scatter x1, waiting for transfers between devices, body(): lax.psum_scatter(jnp.einsum('pte,ed->tpd', context, wout_dec, preferred_e...  13.6 us
    ppermute x2, waiting for transfers between devices, from_behind(): lax.ppermute(value, axis, [(i, (i + by) % devices) for i in range(devices)])  11.3 us
    unnamed x23, local copies, waits for them, and re-layouts  11.3 us
    all_gather x1, waiting for transfers between devices, body(): lax.all_gather(enc_query, 'batch', axis=0, tiled=True)  9.63 us
    ppermute x2, starting transfers between devices, from_behind(): lax.ppermute(value, axis, [(i, (i + by) % devices) for i in range(devices)])  6.9 us
    all_gather x1, waiting for transfers between devices, body(): lax.all_gather(dec_query, 'batch', axis=0, tiled=True)  5.6 us
  transfers between devices with their start and end apart: 11, of which 8 were waited for; matrix products, arithmetic and copies ran while one was open for 25% of the time, Pallas kernels for 0%

commit v1 on v0

--- a/solution.py
+++ b/solution.py
@@ -6,6 +6,19 @@
 
 HEAD_ENC = 32
 HEAD_DEC = 64
+
+
+def collect(array, axis, dim):
+    ways = lax.axis_size(axis)
+    up = [(d, (d + 1) % ways) for d in range(ways)]
+    down = [(d, (d - 1) % ways) for d in range(ways)]
+    earlier, later = ([array], [array])
+    for _ in range(ways // 2):
+        earlier.append(lax.ppermute(earlier[-1], axis, up))
+    for _ in range((ways - 1) // 2):
+        later.append(lax.ppermute(later[-1], axis, down))
+    line = jnp.concatenate([*earlier[::-1], *later[1:]], axis=dim)
+    return jnp.roll(line, (lax.axis_index(axis) - ways // 2) * array.shape[dim], axis=dim)
 
 
 def from_behind(value, axis, by):
@@ -112,7 +125,7 @@
         jnp.zeros((pages_here, heads_dec, text_len, HEAD_DEC), jnp.float32),
     )
     carried = start_state
-    shard_rows = lax.all_gather(page_kv, "tile", axis=1, tiled=True)
+    shard_rows = collect(page_kv, "tile", 1)
     count = shard_rows.shape[1] // own_rows
     grouped = max(
         (

time: 200 us -> 184 us (0.920)
  waiting for transfers between devices: 121 us -> 98.1 us
  starting transfers between devices: 7.43 us -> 12.8 us
    all_gather x1 -> x0, waiting for transfers between devices: 50.8 us -> none  [body(): shard_rows = lax.all_gather(page_kv, 'tile', axis=1, tiled=True)]
    ppermute x0 -> x3, waiting for transfers between devices: none -> 35.4 us  [the longest x2 26.4 us: collect(): earlier.append(lax.ppermute(earlier[-1], axis, up))]
    all_gather x1, waiting for transfers between devices: 5.6 us -> 0.01 us  [body(): lax.all_gather(dec_query, 'batch', axis=0, tiled=True)]
    ppermute x0 -> x3, starting transfers between devices: none -> 5.41 us  [the longest x1 3.87 us: collect(): later.append(lax.ppermute(later[-1], axis, down))]
    unnamed x23 -> x24, local copies, waits for them, and re-layouts: 11.3 us -> 11.5 us
  transfers between devices with their start and end apart: 11 -> 13, of which waited for: 8 -> 9; matrix products, arithmetic and copies ran while one was open for 25% -> 28% of each run, Pallas kernels for 0% -> 0%
where the time goes in v1:
time: 184 us; the launch traced here: 183 us
  waiting for transfers between devices  98.1 us (53%)
  matrix products  25.8 us (14%)
  local copies, waits for them, and re-layouts  23.3 us (13%)
  between operations  14.6 us (8%)
  starting transfers between devices  12.8 us (7%)
  other arithmetic  8.39 us (5%)
    ppermute x2, waiting for transfers between devices, collect(): earlier.append(lax.ppermute(earlier[-1], axis, up))  26.4 us
    psum x1, waiting for transfers between devices, body(): lax.psum(partial_proj.astype(jnp.bfloat16), 'mp').astype(jnp.float32)  25.2 us
    reduce_scatter x1, waiting for transfers between devices, body(): lax.psum_scatter(jnp.einsum('pte,ed->tpd', context, wout_dec, preferred_e...  13.4 us
    unnamed x24, local copies, waits for them, and re-layouts  11.5 us
    ppermute x2, waiting for transfers between devices, from_behind(): lax.ppermute(value, axis, [(i, (i + by) % devices) for i in range(devices)])  11.3 us
    all_gather x1, waiting for transfers between devices, body(): lax.all_gather(enc_query, 'batch', axis=0, tiled=True)  9.63 us
    ppermute x1, waiting for transfers between devices, collect(): later.append(lax.ppermute(later[-1], axis, down))  9 us
    ppermute x2, starting transfers between devices, from_behind(): lax.ppermute(value, axis, [(i, (i + by) % devices) for i in range(devices)])  6.9 us
  transfers between devices with their start and end apart: 13, of which 9 were waited for; matrix products, arithmetic and copies ran while one was open for 28% of the time, Pallas kernels for 0%

profile of v1, /device:TPU:0, one launch (start us, length us, event | category | flops | bytes accessed | tf_op | source)
XLA Modules:
  0.0 183.0 jit_solution(17881215501222349289)
XLA Ops:
  7.2 0.7 all-gather.9.cloned.1.call-update
  7.9 0.7 all-gather.7.cloned.1.call-update
  8.7 0.7 all-gather.11.cloned.1.call-update
  9.4 1.2 fusion.80
  10.6 5.1 %collective-permute-start = (bf16[1,6,24,1024]{3,2,1,0:T(8,128)(2,1)S(1)}, bf16[1,6,24,1024]{3,2,1,0:T(8,128)(2,1)S(1)}, u32[]{:S(2)}, u32[]{:S(2)}) collective-permute-start(bf16[1,6,24,1024]{3,2,1,0:T(8,128)(2,1)S(1)} %get-tuple-element.29), channel_id=1, source_target_pairs={{0,12},{4,0},{8,4},{12,8},{1,13},{5,1},{9,5},{13,9},{2,14},{6,2},{... | collective-permute-start | bytes 884744 | tf_op jit(solution)/shard_map/ppermute | solution.py:26
  16.1 0.7 broadcast_compare_fusion
  16.8 5.1 %collective-permute-done = bf16[1,6,24,1024]{3,2,1,0:T(8,128)(2,1)S(1)} collective-permute-done((bf16[1,6,24,1024]{3,2,1,0:T(8,128)(2,1)S(1)}, bf16[1,6,24,1024]{3,2,1,0:T(8,128)(2,1)S(1)}, u32[]{:S(2)}, u32[]{:S(2)}) %collective-permute-start) | collective-permute-done | bytes 294944 | tf_op jit(solution)/shard_map/ppermute | solution.py:26
  22.4 0.4 all-gather.9.cloned.1.call-done
  22.9 2.1 %copy.40 = bf16[128,8,2,512]{3,1,2,0:T(8,128)(2,1)S(1)} copy(bf16[128,8,2,512]{3,2,1,0:T(2,128)(2,1)} %bitcast.102) | data formatting | bytes 4194304
  25.0 9.6 %all-gather.7.cloned.1.call-done = bf16[1024,512]{1,0:T(8,128)(2,1)} async-done(((bf16[512,512]{1,0:T(8,128)(2,1)}), bf16[1024,512]{1,0:T(8,128)(2,1)}) %all-gather.7.cloned.1.call-update) | async-done | bytes 1048592 | tf_op jit(solution)/shard_map/all_gather | solution.py:44
  34.6 2.4 %fusion.12 = bf16[1,12,24,1536]{3,2,1,0:T(8,128)(2,1)S(1)} fusion(bf16[1024,1024]{1,0:T(8,128)(2,1)S(1)} %bitcast.104, bf16[1024,512]{1,0:T(8,128)(2,1)} %all-gather.7.cloned.1.call-done, bf16[6,24,1024]{2,1,0:T(8,128)(2,1)S(1)} %bitcast.106, bf16[6,24,1024]{2,1,0:T(8,128)(2,1)S(1)} %get-tuple-element.28, f32[12,24]{1,0:T(8,128)S(1)} %add_sqrt_fusion.1, ...), kind=kOutput, calls=%fused_computation.17 | convolution fusion | flops 914178048 | bytes 4622592 | tf_op jit(solution)/shard_map/prcd,de->prce/dot_general | solution.py:61
  37.3 1.1 pad_maximum_fusion
  38.4 3.7 %reshape.311 = bf16[1,12,2,12,3,16,32]{6,5,4,3,2,1,0:T(8,128)(2,1)S(1)} reshape(bf16[1,12,24,1536]{3,2,1,0:T(8,128)(2,1)} %pad_maximum_fusion) | data formatting | bytes 1769472 | tf_op jit(solution)/shard_map/reshape | solution.py:66
  42.0 0.6 copy.26
  42.7 0.6 fusion.79
  43.3 1.7 copy.39
  45.0 1.0 copy.38
  46.1 1.0 copy.37
  47.1 5.0 %fusion.81 = (f32[2,16,144]{2,1,0:T(8,128)S(1)}, f32[2,16,144,144]{2,3,1,0:T(8,128)}) fusion(pred[2,144,144]{1,2,0:T(8,128)(4,1)} %broadcast_compare_fusion, bf16[1,2,144,1,16,32]{2,5,4,1,3,0:T(8,128)(2,1)} %copy.39, bf16[1,2,144,1,16,32]{2,5,4,1,3,0:T(8,128)(2,1)S(1)} %copy.38), kind=kOutput, calls=%fused_computation.113 | convolution fusion | flops 45121680 | bytes 3303936 | tf_op jit(solution)/shard_map/sub | solution.py:88
  52.1 2.8 %fusion.24 = bf16[1,2,144,16,32]{2,4,3,1,0:T(8,128)(2,1)S(1)} fusion(f32[2,16,144,144]{2,3,1,0:T(8,128)} %get-tuple-element.33, f32[2,16,144]{2,1,0:T(8,128)S(1)} %get-tuple-element.32, bf16[1,2,144,1,16,32]{2,5,4,1,3,0:T(8,128)(2,1)S(1)} %copy.37), kind=kOutput, calls=%fused_computation.38 | convolution fusion | flops 43941888 | bytes 3262464 | tf_op jit(solution)/shard_map/pnhqk,pnkhd->pnqhd/dot_general | solution.py:90
  54.9 1.1 copy.31
  56.0 0.9 reshape.316
  57.1 1.8 collective-permute-start.1
  58.9 6.2 %collective-permute-done.1 = bf16[1,6,24,512]{3,2,1,0:T(8,128)(2,1)S(1)} collective-permute-done((bf16[1,6,24,512]{3,2,1,0:T(8,128)(2,1)S(1)}, bf16[1,6,24,512]{3,2,1,0:T(8,128)(2,1)S(1)}, u32[]{:S(2)}, u32[]{:S(2)}) %collective-permute-start.1) | collective-permute-done | bytes 147488 | tf_op jit(solution)/shard_map/ppermute | solution.py:26
  65.1 2.5 %fusion.20 = bf16[1,12,24,1024]{3,2,1,0:T(8,128)(2,1)} fusion(bf16[512,1024]{1,0:T(8,128)(2,1)} %all-gather.11.cloned.1.call-done, bf16[1,12,18,512]{3,2,1,0:T(8,128)(2,1)S(1)} %bitcast.100, bf16[1,12,6,512]{3,2,1,0:T(8,128)(2,1)S(1)} %slice.63, bf16[1,6,24,512]{3,2,1,0:T(8,128)(2,1)S(1)} %collective-permute-done.1), kind=kOutput, calls=%fused_computation.34 | convolution fusion | flops 303169536 | bytes 2080768 | tf_op jit(solution)/shard_map/prce,ed->prcd/dot_general | solution.py:98
  67.7 0.5 all-gather.13.cloned.1.call-update
  68.5 3.5 %copy.41 = bf16[128,8,2,512]{3,1,2,0:T(8,128)(2,1)} copy(bf16[128,8,2,512]{3,2,1,0:T(2,128)(2,1)} %bitcast.101) | data formatting | bytes 4194304
  72.0 25.2 %all-reduce.2.cloned.1.call-done = bf16[1,12,24,1024]{3,2,1,0:T(8,128)(2,1)} async-done(((bf16[1,12,24,1024]{3,2,1,0:T(8,128)(2,1)}), bf16[1,12,24,1024]{3,2,1,0:T(8,128)(2,1)}) %all-reduce.2.cloned.1.call-update) | async-done | bytes 589840 | tf_op jit(solution)/shard_map/psum | solution.py:101
  97.1 1.5 convert_reduce_fusion
  98.6 0.3 fusion.29
  99.2 0.8 fusion.21
  100.0 1.5 collective-permute-start.2
  101.8 15.1 %collective-permute-done.2 = bf16[1,288,1024]{2,1,0:T(8,128)(2,1)S(1)} collective-permute-done((bf16[1,288,1024]{2,1,0:T(8,128)(2,1)S(1)}, bf16[1,288,1024]{2,1,0:T(8,128)(2,1)S(1)}, u32[]{:S(2)}, u32[]{:S(2)}) %collective-permute-start.2) | collective-permute-done | bytes 589856 | tf_op jit(solution)/shard_map/ppermute | solution.py:17
  117.2 3.9 %collective-permute-start.4 = (bf16[1,288,1024]{2,1,0:T(8,128)(2,1)S(1)}, bf16[1,288,1024]{2,1,0:T(8,128)(2,1)S(1)}, u32[]{:S(2)}, u32[]{:S(2)}) collective-permute-start(bf16[1,288,1024]{2,1,0:T(8,128)(2,1)S(1)} %fusion.21), channel_id=1, source_target_pairs={{0,12},{4,0},{8,4},{12,8},{1,13},{5,1},{9,5},{13,9},{2,14},{6,2},{... | collective-permute-start | bytes 1769480 | tf_op jit(solution)/shard_map/ppermute | solution.py:19
  121.1 1.7 convolution_convert_fusion.3
  122.8 0.8 copy.33
  123.6 11.3 %collective-permute-done.3 = bf16[1,288,1024]{2,1,0:T(8,128)(2,1)S(1)} collective-permute-done((bf16[1,288,1024]{2,1,0:T(8,128)(2,1)S(1)}, bf16[1,288,1024]{2,1,0:T(8,128)(2,1)S(1)}, u32[]{:S(2)}, u32[]{:S(2)}) %collective-permute-start.3) | collective-permute-done | bytes 589856 | tf_op jit(solution)/shard_map/ppermute | solution.py:17
  135.1 9.0 %collective-permute-done.4 = bf16[1,288,1024]{2,1,0:T(8,128)(2,1)S(1)} collective-permute-done((bf16[1,288,1024]{2,1,0:T(8,128)(2,1)S(1)}, bf16[1,288,1024]{2,1,0:T(8,128)(2,1)S(1)}, u32[]{:S(2)}, u32[]{:S(2)}) %collective-permute-start.4) | collective-permute-done | bytes 589856 | tf_op jit(solution)/shard_map/ppermute | solution.py:19
  144.3 1.0 constant_dynamic-slice_fusion
  145.3 0.7 copy.34
  146.0 2.5 %multiply_reduce_fusion = (f32[8,256]{1,0:T(8,128)S(1)}, f32[8,256,1152]{2,1,0:T(8,128)S(1)}) fusion(bf16[256,8,64]{0,2,1:T(8,128)(2,1)} %bitcast.108, bf16[1152,8,64]{0,2,1:T(8,128)(2,1)S(1)} %bitcast.98), kind=kOutput, calls=%fused_computation.2 | convolution fusion | flops 306706432 | bytes 10887168 | tf_op jit(solution)/shard_map/while/body/eval_jaxpr/pqhd,pkhd->phqk/dot_general | solution.py:146
  148.5 1.9 %fusion.1 = f32[8,256]{1,0:T(8,128)S(1)} fusion(f32[8,256,1152]{2,1,0:T(8,128)S(1)} %get-tuple-element.35, f32[8,256]{1,0:T(8,128)S(1)} %get-tuple-element.34), kind=kLoop, calls=%fused_computation.3 | loop fusion | flops 7075840 | bytes 9453568 | tf_op jit(solution)/shard_map/while/body/eval_jaxpr/reduce_sum | solution.py:152
  150.4 1.7 copy-done
  152.1 0.7 copy.35
  152.9 5.6 %fusion.41 = bf16[8,256,64]{1,2,0:T(8,128)(2,1)S(1)} fusion(bf16[1152,8,64]{0,2,1:T(8,128)(2,1)S(1)} %bitcast.105, f32[8,256,1152]{2,1,0:T(8,128)} %copy-done, f32[8,256]{1,0:T(8,128)S(1)} %get-tuple-element.34, f32[8,256]{1,0:T(8,128)S(1)} %get-tuple-element.31, f32[8,256]{1,0:T(8,128)S(1)} %get-tuple-element.30), kind=kOutput, calls=%fused_computation.53 | convolution fusion | flops 309460992 | bytes 10903552 | tf_op jit(solution)/shard_map/while/body/eval_jaxpr/phqk,pkhd->phqd/dot_general | solution.py:153
  158.5 2.5 %fusion.25 = bf16[256,1,1024]{2,0,1:T(8,128)(2,1)} fusion(bf16[256,512]{0,1:T(8,128)(2,1)S(1)} %bitcast.110, bf16[512,1024]{1,0:T(8,128)(2,1)} %all-gather.17.cloned.1.call-done), kind=kOutput, calls=%fused_computation.39 | convolution fusion | flops 268697600 | bytes 1835008 | tf_op jit(solution)/shard_map/pte,ed->tpd/dot_general | solution.py:170
  161.0 13.4 %reduce-scatter.2.cloned.1.call-done = bf16[128,1,1024]{2,0,1:T(8,128)(2,1)} async-done(((bf16[256,1,1024]{2,0,1:T(8,128)(2,1)}), bf16[128,1,1024]{2,0,1:T(8,128)(2,1)}) %reduce-scatter.2.cloned.1.call-update) | async-done | bytes 262160 | tf_op jit(solution)/shard_map/reduce_scatter | solution.py:169
  174.4 1.7 fusion.51
  (61 shorter events, 2.8 us)
Async XLA Ops:
  7.2 15.7 %all-gather.9.cloned.1.call-start = ((), (), s32[]{:S(2)}) async-start(), calls=%async_computation.2 | async-start | bytes 3145728 | tf_op jit(solution)/shard_map/all_gather | solution.py:45
  7.9 26.7 %all-gather.7.cloned.1.call-start = ((), (), s32[]{:S(2)}) async-start(), calls=%async_computation.1 | async-start | bytes 1572864 | tf_op jit(solution)/shard_map/all_gather | solution.py:44
  8.6 50.3 %all-gather.11.cloned.1.call-start = ((), (), s32[]{:S(2)}) async-start(), calls=%async_computation.3 | async-start | bytes 1572864 | tf_op jit(solution)/shard_map/all_gather | solution.py:46
  9.4 59.1 %all-gather.15.cloned.1.call-start = ((), (), s32[]{:S(2)}) async-start(), calls=%async_computation.6 | async-start | bytes 3145728 | tf_op jit(solution)/shard_map/all_gather | solution.py:48
  10.6 11.4 %collective-permute-start = (bf16[1,6,24,1024]{3,2,1,0:T(8,128)(2,1)S(1)}, bf16[1,6,24,1024]{3,2,1,0:T(8,128)(2,1)S(1)}, u32[]{:S(2)}, u32[]{:S(2)}) collective-permute-start(bf16[1,6,24,1024]{3,2,1,0:T(8,128)(2,1)S(1)} %get-tuple-element.29), channel_id=1, source_target_pairs={{0,12},{4,0},{8,4},{12,8},{1,13},{5,1},{9,5},{13,9},{2,14},{6,2},{... | collective-permute-start | bytes 884744 | tf_op jit(solution)/shard_map/ppermute | solution.py:26
  15.7 81.4 %all-reduce.2.cloned.1.call-start = ((), (), s32[]{:S(2)}) async-start(), calls=%async_computation.4 | async-start | bytes 1179648 | tf_op jit(solution)/shard_map/psum | solution.py:101
  57.1 40.0 %copy-start.4 = (bf16[1,12,24,1024]{3,2,1,0:T(8,128)(2,1)S(1)}, bf16[1,12,24,1024]{3,2,1,0:T(8,128)(2,1)}, u32[]{:S(2)}) copy-start(bf16[1,12,24,1024]{3,2,1,0:T(8,128)(2,1)} %param.8) | copy-start | bytes 1769476
  57.1 8.0 %collective-permute-start.1 = (bf16[1,6,24,512]{3,2,1,0:T(8,128)(2,1)S(1)}, bf16[1,6,24,512]{3,2,1,0:T(8,128)(2,1)S(1)}, u32[]{:S(2)}, u32[]{:S(2)}) collective-permute-start(bf16[1,6,24,512]{3,2,1,0:T(8,128)(2,1)S(1)} %fusion.71), channel_id=1, source_target_pairs={{0,4},{4,8},{8,12},{12,0},{1,5},{5,9},{9,13},{13,1},{2,6},{6,10},{... | collective-permute-start | bytes 442376 | tf_op jit(solution)/shard_map/ppermute | solution.py:26
  67.6 53.5 %all-gather.13.cloned.1.call-start = ((), (), s32[]{:S(2)}) async-start(), calls=%async_computation.5 | async-start | bytes 1572864 | tf_op jit(solution)/shard_map/all_gather | solution.py:47
  68.2 90.3 %all-gather.17.cloned.1.call-start = ((), (), s32[]{:S(2)}) async-start(), calls=%async_computation.7 | async-start | bytes 1572864 | tf_op jit(solution)/shard_map/all_gather | solution.py:49
  97.1 2.0 %copy-start.5 = (bf16[128,8,2,512]{3,1,2,0:T(8,128)(2,1)S(1)}, bf16[128,8,2,512]{3,1,2,0:T(8,128)(2,1)}, u32[]{:S(2)}) copy-start(bf16[128,8,2,512]{3,1,2,0:T(8,128)(2,1)} %copy.41) | copy-start | bytes 6291460
  98.6 2.9 %copy-start.1 = (bf16[1,12,24,1024]{3,2,1,0:T(8,128)(2,1)}, bf16[1,12,24,1024]{3,2,1,0:T(8,128)(2,1)S(1)}, u32[]{:S(2)}) copy-start(bf16[1,12,24,1024]{3,2,1,0:T(8,128)(2,1)S(1)} %get-tuple-element.15) | copy-start | bytes 1769476
  98.9 2.7 %copy-start.2 = (bf16[1,256,1024]{2,1,0:T(8,128)(2,1)S(1)}, bf16[1,256,1024]{2,1,0:T(8,128)(2,1)}, u32[]{:S(2)}) copy-start(bf16[1,256,1024]{2,1,0:T(8,128)(2,1)} %param.9) | copy-start | bytes 1572868
  100.0 16.9 %collective-permute-start.2 = (bf16[1,288,1024]{2,1,0:T(8,128)(2,1)S(1)}, bf16[1,288,1024]{2,1,0:T(8,128)(2,1)S(1)}, u32[]{:S(2)}, u32[]{:S(2)}) collective-permute-start(bf16[1,288,1024]{2,1,0:T(8,128)(2,1)S(1)} %fusion.21), channel_id=1, source_target_pairs={{0,4},{4,8},{8,12},{12,0},{1,5},{5,9},{9,13},{13,1},{2,6},{6,10},{... | collective-permute-start | bytes 1769480 | tf_op jit(solution)/shard_map/ppermute | solution.py:17
  101.5 72.9 %reduce-scatter.2.cloned.1.call-start = ((), (), s32[]{:S(2)}) async-start(), calls=%async_computation.8 | async-start | bytes 786432 | tf_op jit(solution)/shard_map/reduce_scatter | solution.py:169
  116.9 18.1 %collective-permute-start.3 = (bf16[1,288,1024]{2,1,0:T(8,128)(2,1)S(1)}, bf16[1,288,1024]{2,1,0:T(8,128)(2,1)S(1)}, u32[]{:S(2)}, u32[]{:S(2)}) collective-permute-start(bf16[1,288,1024]{2,1,0:T(8,128)(2,1)S(1)} %collective-permute-done.2), channel_id=1, source_target_pairs={{0,4},{4,8},{8,12},{12,0},{1,5},{5,9},{9,13},{13,1},{2,6},{6,10},{... | collective-permute-start | bytes 1769480 | tf_op jit(solution)/shard_map/ppermute | solution.py:17
  117.2 26.9 %collective-permute-start.4 = (bf16[1,288,1024]{2,1,0:T(8,128)(2,1)S(1)}, bf16[1,288,1024]{2,1,0:T(8,128)(2,1)S(1)}, u32[]{:S(2)}, u32[]{:S(2)}) collective-permute-start(bf16[1,288,1024]{2,1,0:T(8,128)(2,1)S(1)} %fusion.21), channel_id=1, source_target_pairs={{0,12},{4,0},{8,4},{12,8},{1,13},{5,1},{9,5},{13,9},{2,14},{6,2},{... | collective-permute-start | bytes 1769480 | tf_op jit(solution)/shard_map/ppermute | solution.py:19
  148.5 3.6 %copy-start = (f32[8,256,1152]{2,1,0:T(8,128)}, f32[8,256,1152]{2,1,0:T(8,128)S(1)}, u32[]{:S(2)}) copy-start(f32[8,256,1152]{2,1,0:T(8,128)S(1)} %get-tuple-element.35) | copy-start | bytes 28311556
  152.9 21.6 %copy-start.3 = (bf16[1,256,1024]{2,1,0:T(8,128)(2,1)S(1)}, bf16[1,256,1024]{2,1,0:T(8,128)(2,1)}, u32[]{:S(2)}) copy-start(bf16[1,256,1024]{2,1,0:T(8,128)(2,1)} %param.9) | copy-start | bytes 1572868
Sparse Core Ops, SparseCore 0:
  9.5 13.2 all-gather.8
  24.4 10.1 all-gather.6
  36.2 10.1 all-gather.10
  47.8 11.7 all-gather.14
  67.7 29.3 all-reduce.1
  98.6 9.0 all-gather.12
  109.3 10.1 all-gather.16
  161.1 13.2 reduce-scatter.1
